TPU v7x, 32 devices: a whole 2x2x4 slice. The times are simulated.
32 devices in a mesh: dp: 16 (over z, y, x), band: 2 (over core).
Axes of the slice: x: 2, y: 2, z: 4, core: 2. Of those that a mesh axis runs over, the one named last changes fastest.
Arguments:
- spectra: bfloat16 [224, 1024, 256], P('band', 'dp'), may hold values from -6 to 6
- first_spectral_weight: bfloat16 [3, 256, 256], replicated, may hold values from -0.21875 to 0.21875
- second_spectral_weight: bfloat16 [3, 256, 256], replicated, may hold values from -0.21875 to 0.21875
- patch_w: float32 [4, 256], replicated, may hold values from -3 to 3
- cotangent: bfloat16 [224, 256, 256], P('band', 'dp'), may hold values from -6 to 6
Outputs:
- spectra_gradient: bfloat16 [224, 1024, 256], P('band', 'dp')
- grad_first: float32 [256, 3, 256], P('dp')
- grad_second: float32 [256, 3, 256], P('dp')
- grad_patch: float32 [4, 256], replicated
All inputs are finite; a program needn't handle non-finite values.
Results may differ from a plain program's by a relative error of at most 0.014.
Values may be sent and summed in bfloat16 or wider, within the bound.
A program may use at most 128 MiB of HBM per device.

v0:
```python
import functools
import math

import jax
import jax.numpy as jnp
from jax import lax
from jax.experimental import pallas as pl
from jax.experimental.pallas import tpu as pltpu
from jax.sharding import PartitionSpec as P

D1 = 1
D2 = 2
HZ = 1 + 2 * D2
HX = HZ + D1
HC = 1 + D2
MESH = pl.DeviceIdType.MESH
F32 = jnp.float32
BF16 = jnp.bfloat16
G0 = math.sqrt(2.0 / math.pi)
G1 = 0.044715 * G0


def divisor(n, most):
    return max(i for i in range(1, min(n, most) + 1) if n % i == 0)


def gelu_terms(v):
    sq = v * v
    p = 0.5 + 0.5 * jnp.tanh(v * (G0 + G1 * sq))
    u = v * p
    s = p + u * (1.0 - p) * (2.0 * G0 + (6.0 * G1) * sq)
    return u, s


def dot(a, b):
    return jnp.dot(a, b, preferred_element_type=F32)


def dot_rows(a, b):
    return lax.dot_general(a, b, (((0,), (0,)), ((), ())), preferred_element_type=F32)


def stacked(ref, starts, n):
    c = ref.shape[-1]
    return jnp.concatenate([ref[pl.ds(s, n)].reshape(-1, c) for s in starts], axis=-1)


def copy_in(pairs, sems):
    copies = [pltpu.make_async_copy(a, b, sems.at[i]) for i, (a, b) in enumerate(pairs)]
    for c in copies:
        c.start()
    return copies


def turn_weights(w1_ref, w2_ref, w1t, w2t):
    C = w1_ref.shape[-1]
    for k in range(3):
        w1t[pl.ds(k * C, C), :] = w1_ref[k].T
        w2t[pl.ds(k * C, C), :] = w2_ref[k].T


def first_layer(me, nb, early, late, xe, w1_ref, pw, hs_a, hs_b, u_s, s_s, z1e):
    n1, Q, C = z1e.shape
    L = n1 - 2 * HZ
    H = C // 2
    b1 = min(8, n1)
    steps = (n1 + b1 - 1) // b1
    edge = min((HX + L - 2 * D1) // b1, steps - 1)

    def chunk(at):
        return jnp.minimum(lax.rem(at + 1, steps) * b1, n1 - b1)

    def mix(at, hs):
        s = chunk(at)
        h = dot(stacked(xe, [s, s + D1, s + 2 * D1], b1), w1_ref[...].reshape(3 * C, C))
        for t in range(2):
            hs[t] = h[:, t * H:(t + 1) * H]

    def activate(at, hs):
        s = chunk(at)
        for t in range(2):
            z = None
            for j in range(4):
                v = hs[t, pl.ds(j, b1 * Q, stride=4), :]
                u, sl = gelu_terms(v)
                u_s[j, pl.ds(s, b1), :, t * H:(t + 1) * H] = u.reshape(b1, Q, H)
                s_s[j, pl.ds(s, b1), :, t * H:(t + 1) * H] = sl.reshape(b1, Q, H)
                term = u * pw[j:j + 1, t * H:(t + 1) * H]
                z = term if z is None else z + term
            z1e[pl.ds(s, b1), :, t * H:(t + 1) * H] = z.reshape(b1, Q, H).astype(BF16)

    mix(0, hs_a)
    pairs = (steps - 1) // 2

    @pl.loop(0, pairs)
    def _(i):
        at = 2 * i

        @pl.when(i == 0)
        def _():
            early()

        @pl.when(i == max((edge - 2) // 2, 0))
        def _():
            late()

        mix(at + 1, hs_b)
        activate(at, hs_a)
        mix(at + 2, hs_a)
        activate(at + 1, hs_b)

    if steps % 2 == 0:
        mix(steps - 1, hs_b)
    activate(2 * pairs, hs_a)
    if steps % 2 == 0:
        activate(steps - 1, hs_b)

    @pl.when(me == 0)
    def _():
        z1e[pl.ds(0, HZ)] = jnp.zeros((HZ, Q, C), BF16)

    @pl.when(me == nb - 1)
    def _():
        z1e[pl.ds(HZ + L, HZ)] = jnp.zeros((HZ, Q, C), BF16)


def second_layer(z1e, ce, w2_ref, dh2e, acc2):
    n2, Q, C = ce.shape
    L = n2 - 2 * HC
    b2 = min(16, n2)
    bg = divisor(L, b2)
    steps, gsteps = (n2 + b2 - 1) // b2, L // bg
    acc2[...] = jnp.zeros_like(acc2)

    def delta(i):
        s = jnp.minimum(i * b2, n2 - b2)
        h = dot(stacked(z1e, [s, s + D2, s + 2 * D2], b2), w2_ref[...].reshape(3 * C, C))
        sl = gelu_terms(h)[1]
        d = ce[pl.ds(s, b2)].reshape(b2 * Q, C).astype(F32) * sl
        dh2e[pl.ds(s, b2)] = d.astype(BF16).reshape(b2, Q, C)

    def weight_gradient(i):
        b = i * bg
        d = dh2e[pl.ds(b + HC, bg)].reshape(bg * Q, C)
        acc2[...] += dot_rows(d, stacked(z1e, [b + HZ - D2, b + HZ, b + HZ + D2], bg))

    lead = min(2, steps)
    both = min(steps, gsteps + lead)
    pl.loop(0, lead)(delta)

    @pl.loop(lead, both)
    def _(i):
        weight_gradient(i - lead)
        delta(i)

    pl.loop(both, steps)(delta)
    pl.loop(both - lead, gsteps)(weight_gradient)


def first_delta(me, nb, dh2e, w2t, pw, u_s, s_s, hs, gpa, dh1e, xe, acc1):
    n3, px, C = dh1e.shape
    L = n3 - 2
    Q = px // 4
    H = C // 2
    gpa[...] = jnp.zeros_like(gpa)
    acc1[...] = jnp.zeros_like(acc1)
    b3 = min(8, n3)
    bx = divisor(L, b3)
    steps, gsteps = (n3 + b3 - 1) // b3, L // bx

    def delta(i):
        s = jnp.minimum(i * b3, n3 - b3)
        o = HC - 1
        dz = dot(stacked(dh2e, [s + o + D2, s + o, s + o - D2], b3), w2t[...])
        band = s + lax.broadcasted_iota(jnp.int32, (b3, Q, 1), 0).reshape(b3 * Q, 1)
        own = (band >= jnp.maximum(1, i * b3)) & (band <= L)
        dzo = jnp.where(own, dz, 0.0)
        for t in range(2):
            cols = slice(t * H, (t + 1) * H)
            for j in range(4):
                u = u_s[j, pl.ds(s + HZ - 1, b3), :, cols].reshape(b3 * Q, H)
                sl = s_s[j, pl.ds(s + HZ - 1, b3), :, cols].reshape(b3 * Q, H)
                hs[t, pl.ds(j, b3 * Q, stride=4), :] = dz[:, cols] * pw[j:j + 1, cols] * sl
                gpa[j, :, cols] += jnp.sum((dzo[:, cols] * u).reshape(-1, 8, H), axis=0)
        for t in range(2):
            cols = slice(t * H, (t + 1) * H)
            dh1e[pl.ds(s, b3), :, cols] = hs[t].astype(BF16).reshape(b3, px, H)

    def weight_gradient(i):
        b = i * bx
        d = dh1e[pl.ds(b + 1, bx)].reshape(bx * px, C)
        acc1[...] += dot_rows(d, stacked(xe, [b + HX - D1, b + HX, b + HX + D1], bx))

    lead = min(2, steps)
    both = min(steps, gsteps + lead)
    pl.loop(0, lead)(delta)

    @pl.loop(lead, both)
    def _(i):
        weight_gradient(i - lead)
        delta(i)

    pl.loop(both, steps)(delta)

    @pl.when(me == 0)
    def _():
        dh1e[0] = jnp.zeros((px, C), BF16)

    @pl.when(me == nb - 1)
    def _():
        dh1e[L + 1] = jnp.zeros((px, C), BF16)

    pl.loop(both - lead, gsteps)(weight_gradient)


def input_gradient(dh1e, w1t, dx_ref, hooks, finish):
    L, px, C = dx_ref.shape
    bx = divisor(L, 8)
    steps = L // bx

    @pl.loop(0, steps)
    def _(i):
        for at, hook in hooks:
            pl.when(i == min(at, steps - 1))(hook)
        b = i * bx
        g = dot(stacked(dh1e, [b + 1 + D1, b + 1, b + 1 - D1], bx), w1t[...])
        dx_ref[pl.ds(b, bx)] = g.astype(BF16).reshape(bx, px, C)
        finish(pl.ds(b, bx))


def local_kernel(
    nb,
    x_hbm, xlo_hbm, xhi_hbm, cot_hbm, clo_hbm, chi_hbm, w1_ref, w2_ref, pw_ref,
    dx_ref, g_ref, gp_ref,
    xe, ce, z1e, dh2e, dh1e, u_s, s_s, hs, hs_b, w1t, w2t, acc1, acc2, gpa, sems,
):
    L, px, C = x_hbm.shape
    me = lax.axis_index("band")
    copies = copy_in([
        (xlo_hbm, xe.at[pl.ds(0, HX)]),
        (x_hbm, xe.at[pl.ds(HX, L)]),
        (xhi_hbm, xe.at[pl.ds(HX + L, HX)]),
        (clo_hbm, ce.at[pl.ds(0, HC)]),
        (cot_hbm, ce.at[pl.ds(HC, L)]),
        (chi_hbm, ce.at[pl.ds(HC + L, HC)]),
    ], sems)
    turn_weights(w1_ref, w2_ref, w1t, w2t)
    for c in copies:
        c.wait()
    pw = pw_ref[...]
    nothing = lambda *_: None
    first_layer(me, nb, nothing, nothing, xe, w1_ref, pw, hs, hs_b, u_s, s_s, z1e)
    second_layer(z1e, ce, w2_ref, dh2e, acc2)
    first_delta(me, nb, dh2e, w2t, pw, u_s, s_s, hs, gpa, dh1e, xe, acc1)
    input_gradient(dh1e, w1t, dx_ref, [], nothing)
    g_ref[0] = acc1[...].astype(BF16)
    g_ref[1] = acc2[...].astype(BF16)
    gp_ref[...] = jnp.sum(gpa[...], axis=1)


def local_scratch(L, px, C):
    Q = px // 4
    return [
        pltpu.VMEM((L + 2 * HX, px, C), BF16),
        pltpu.VMEM((L + 2 * HC, Q, C), BF16),
        pltpu.VMEM((L + 2 * HZ, Q, C), BF16),
        pltpu.VMEM((L + 2 * HC, Q, C), BF16),
        pltpu.VMEM((L + 2, px, C), BF16),
        pltpu.VMEM((4, L + 2 * HZ, Q, C), F32),
        pltpu.VMEM((4, L + 2 * HZ, Q, C), F32),
        pltpu.VMEM((2, 8 * px, C // 2), F32),
        pltpu.VMEM((2, 8 * px, C // 2), F32),
        pltpu.VMEM((3 * C, C), BF16),
        pltpu.VMEM((3 * C, C), BF16),
        pltpu.VMEM((C, 3 * C), F32),
        pltpu.VMEM((C, 3 * C), F32),
        pltpu.VMEM((4, 8, C), F32),
        pltpu.SemaphoreType.DMA((6,)),
    ]


def local_pass(nb, x, xlo, xhi, cot, clo, chi, w1, w2, pw):
    L, px, C = x.shape
    Q = px // 4
    any_spec = pl.BlockSpec(memory_space=pl.ANY)
    vm = pl.BlockSpec(memory_space=pltpu.VMEM)
    return pl.pallas_call(
        functools.partial(local_kernel, nb),
        out_shape=(
            jax.ShapeDtypeStruct((L, px, C), BF16),
            jax.ShapeDtypeStruct((2, C, 3 * C), BF16),
            jax.ShapeDtypeStruct((4, C), F32),
        ),
        in_specs=[any_spec] * 6 + [vm] * 3,
        out_specs=[vm] * 3,
        scratch_shapes=local_scratch(L, px, C),
        compiler_params=pltpu.CompilerParams(vmem_limit_bytes=60 * 1024 * 1024),
        name="local_pass",
    )(x, xlo, xhi, cot, clo, chi, w1, w2, pw)


def step_kernel(
    scale, lo_n, hi_n,
    x_hbm, cot_hbm, w1_ref, w2_ref, pw_ref,
    dx_hbm, o_ref, op_ref,
    xe, ce, z1e, dh2e, dh1e, u_s, s_s, hs, hs_b, w1t, w2t, acc1, acc2, gpa, sems,
    gb, r0, s0, r1, s1, r2, fin, rf, p0, p1, p2, q0, hsend, hrecv, ssem, rsem, dxv, dxsem,
):
    L, px, C = x_hbm.shape
    Q = px // 4
    W = 3 * C
    half = W // 2
    R = C // (lo_n * hi_n)
    dp = lax.axis_index("dp")
    core = lax.axis_index("band")
    other = 1 - core
    lo, hi = lax.rem(dp, lo_n), dp // lo_n
    planes = [hi * lo_n + lax.rem(lo + m, lo_n) for m in range(1, lo_n)]
    lines = [lax.rem(hi + m, hi_n) * lo_n + lo for m in range(1, hi_n)]
    order = [lax.rem(lo + m, lo_n) for m in list(range(1, lo_n)) + [0]]
    partner = (dp, other)

    barrier = pltpu.get_barrier_semaphore()
    targets = [partner] + [(d, core) for d in planes + lines]
    for t in targets:
        pl.semaphore_signal(barrier, inc=1, device_id=t, device_id_type=MESH)

    copies = copy_in([(x_hbm, xe.at[pl.ds(HX, L)]), (cot_hbm, ce.at[pl.ds(HC, L)])], sems)
    turn_weights(w1_ref, w2_ref, w1t, w2t)
    xpad = jnp.where(core == 0, 0, HX + L)
    cpad = jnp.where(core == 0, 0, HC + L)
    xe[pl.ds(xpad, HX)] = jnp.zeros((HX, px, C), BF16)
    ce[pl.ds(cpad, HC)] = jnp.zeros((HC, Q, C), BF16)
    for c in copies:
        c.wait()
    pw = pw_ref[...]

    def halos():
        return [
            pltpu.make_async_remote_copy(
                src_ref=src.at[pl.ds(jnp.where(core == 0, L - w, 0), w)],
                dst_ref=dst.at[pl.ds(jnp.where(core == 0, 0, w + L), w)],
                send_sem=hsend.at[i], recv_sem=hrecv.at[i],
                device_id=partner, device_id_type=MESH,
            )
            for i, (src, dst, w) in enumerate([(x_hbm, xe, HX), (cot_hbm, ce, HC)])
        ]

    def early():
        pl.semaphore_wait(barrier, len(targets))
        for c in halos():
            c.start()

    def late():
        for c in halos():
            c.wait()

    def link(i, src, dst, target):
        return pltpu.make_async_remote_copy(
            src_ref=src, dst_ref=dst, send_sem=ssem.at[i], recv_sem=rsem.at[i],
            device_id=target, device_id_type=MESH,
        )

    per = lo_n + (lo_n - 1) + (hi_n - 1) + 1

    def across(q):
        return [link(q * per + m, gb.at[q, other, :, order[m]], r0.at[q, order[m]], partner)
                for m in range(lo_n)]

    def plane(q):
        return [link(q * per + lo_n + m, s0.at[q, m], r1.at[q, m], (planes[m], core))
                for m in range(lo_n - 1)]

    def line(q):
        return [link(q * per + 2 * lo_n - 1 + m, s1.at[q, lax.rem(hi + m + 1, hi_n)], r2.at[q, m],
                     (lines[m], core)) for m in range(hi_n - 1)]

    def ends(q):
        return [link(q * per + per - 1, fin.at[q], rf.at[q], partner)]

    def pairs_p():
        return [link(2 * per, q0.at[0], p0, partner)]

    def plane_p():
        return [link(2 * per + 1 + m, q0.at[1], p1.at[lo], (planes[m], core))
                for m in range(lo_n - 1)]

    def line_p():
        return [link(2 * per + lo_n + m, q0.at[2], p2.at[hi], (lines[m], core))
                for m in range(hi_n - 1)]

    def start(cs):
        for c in cs:
            c.start()

    def arrived(cs):
        for c in cs:
            c.wait_recv()

    def step_a(q, acc):
        for h in range(2):
            gb[q, h] = acc[:, h * half:(h + 1) * half].astype(BF16).reshape(hi_n, lo_n, R, half)
        start(across(q))

    def step_b(q):
        into, out = across(q), plane(q)
        for m in range(lo_n):
            into[m].wait_recv()
            if m == lo_n - 1:
                break
            total = gb[q, core, :, order[m]].astype(F32) + r0[q, order[m]].astype(F32)
            s0[q, m] = total.astype(BF16)
            out[m].start()

    def step_c(q):
        arrived(plane(q))
        own = gb[q, core, :, lo].astype(F32) + r0[q, lo].astype(F32)
        for m in range(lo_n - 1):
            own = own + r1[q, m].astype(F32)
        s1[q] = own.astype(BF16)
        start(line(q))

    def step_d(q):
        arrived(line(q))
        mine = s1[q, hi].astype(F32)
        for m in range(hi_n - 1):
            mine = mine + r2[q, m].astype(F32)
        fin[q] = mine * scale
        start(ends(q))

    def step_e(q):
        arrived(ends(q))
        a, b = fin[q], rf[q]
        row = jnp.concatenate([jnp.where(core == 0, a, b), jnp.where(core == 0, b, a)], axis=-1)
        for k in range(3):
            o_ref[q, k] = row[:, k * C:(k + 1) * C]

    def patch_a():
        q0[0] = jnp.sum(gpa[...], axis=1)
        start(pairs_p())

    def patch_b():
        arrived(pairs_p())
        q0[1] = q0[0] + p0[...]
        p1[lo] = q0[0] + p0[...]
        start(plane_p())

    def patch_c():
        arrived(plane_p())
        total = jnp.sum(p1[...], axis=0)
        q0[2] = total
        p2[hi] = total
        start(line_p())

    def patch_d():
        arrived(line_p())
        op_ref[...] = jnp.sum(p2[...], axis=0) * scale

    first_layer(core, 2, early, late, xe, w1_ref, pw, hs, hs_b, u_s, s_s, z1e)
    second_layer(z1e, ce, w2_ref, dh2e, acc2)
    step_a(1, acc2[...])
    first_delta(core, 2, dh2e, w2t, pw, u_s, s_s, hs, gpa, dh1e, xe, acc1)
    step_a(0, acc1[...])
    patch_a()
    step_b(1)

    def hook_one():
        patch_b()

    def hook_two():
        step_b(0)

    def hook_three():
        step_c(1)
        patch_c()

    def finish(bands):
        pltpu.make_async_copy(dxv.at[bands], dx_hbm.at[bands], dxsem.at[0]).start()

    input_gradient(dh1e, w1t, dxv, [(3, hook_two), (4, hook_one), (11, hook_three)], finish)
    step_c(0)
    step_d(1)
    step_e(1)
    patch_d()
    step_d(0)
    step_e(0)
    for q in range(2):
        for c in across(q) + plane(q) + line(q) + ends(q):
            c.wait_send()
    for c in pairs_p() + plane_p() + line_p():
        c.wait_send()
    pltpu.make_async_copy(dxv, dx_hbm, dxsem.at[0]).wait()


def step_pass(scale, ndp, x, cot, w1, w2, pw):
    L, px, C = x.shape
    R = C // ndp
    half = 3 * C // 2
    lo_n = divisor(ndp, math.isqrt(ndp))
    hi_n = ndp // lo_n
    n = 2 * (2 * lo_n + hi_n - 1) + lo_n + hi_n - 1
    any_spec = pl.BlockSpec(memory_space=pl.ANY)
    vm = pl.BlockSpec(memory_space=pltpu.VMEM)
    return pl.pallas_call(
        functools.partial(step_kernel, scale, lo_n, hi_n),
        out_shape=(
            jax.ShapeDtypeStruct((L, px, C), BF16),
            jax.ShapeDtypeStruct((2, 3, R, C), F32),
            jax.ShapeDtypeStruct((4, C), F32),
        ),
        in_specs=[any_spec] * 2 + [vm] * 3,
        out_specs=[any_spec, vm, vm],
        scratch_shapes=local_scratch(L, px, C) + [
            pltpu.VMEM((2, 2, hi_n, lo_n, R, half), BF16),
            pltpu.VMEM((2, lo_n, hi_n, R, half), BF16),
            pltpu.VMEM((2, lo_n - 1, hi_n, R, half), BF16),
            pltpu.VMEM((2, lo_n - 1, hi_n, R, half), BF16),
            pltpu.VMEM((2, hi_n, R, half), BF16),
            pltpu.VMEM((2, hi_n - 1, R, half), BF16),
            pltpu.VMEM((2, R, half), F32),
            pltpu.VMEM((2, R, half), F32),
            pltpu.VMEM((4, C), F32),
            pltpu.VMEM((lo_n, 4, C), F32),
            pltpu.VMEM((hi_n, 4, C), F32),
            pltpu.VMEM((3, 4, C), F32),
            pltpu.SemaphoreType.DMA((2,)),
            pltpu.SemaphoreType.DMA((2,)),
            pltpu.SemaphoreType.DMA((n,)),
            pltpu.SemaphoreType.DMA((n,)),
            pltpu.VMEM((L, px, C), BF16),
            pltpu.SemaphoreType.DMA((1,)),
        ],
        compiler_params=pltpu.CompilerParams(
            collective_id=0, has_side_effects=True, vmem_limit_bytes=60 * 1024 * 1024
        ),
        name="step_pass",
    )(x, cot, w1, w2, pw)


def hand_over_kernel(n, dx_hbm, o_ref, p_ref, dx_out, o1_out, o2_out, p_out, buf, isem, osem):
    step = dx_hbm.shape[0] // n
    into = [pltpu.make_async_copy(dx_hbm.at[pl.ds(i * step, step)], buf.at[pl.ds(i * step, step)],
                                  isem.at[i]) for i in range(n)]
    out = [pltpu.make_async_copy(buf.at[pl.ds(i * step, step)], dx_out.at[pl.ds(i * step, step)],
                                 osem.at[i]) for i in range(n)]
    for c in into:
        c.start()
    o1_out[...] = o_ref[0]
    o2_out[...] = o_ref[1]
    p_out[...] = p_ref[...]
    for a, b in zip(into, out):
        a.wait()
        b.start()
    for b in out:
        b.wait()


def hand_over(dx, o, p):
    n = divisor(dx.shape[0], 14)
    vm = pl.BlockSpec(memory_space=pltpu.VMEM)
    any_spec = pl.BlockSpec(memory_space=pl.ANY)
    one = jax.ShapeDtypeStruct(o.shape[1:], F32)
    dx, o1, o2, p = pl.pallas_call(
        functools.partial(hand_over_kernel, n),
        out_shape=(jax.ShapeDtypeStruct(dx.shape, dx.dtype), one, one,
                   jax.ShapeDtypeStruct(p.shape, F32)),
        in_specs=[any_spec, vm, vm],
        out_specs=[any_spec, vm, vm, vm],
        scratch_shapes=[pltpu.VMEM(dx.shape, dx.dtype), pltpu.SemaphoreType.DMA((n,)),
                        pltpu.SemaphoreType.DMA((n,))],
        name="hand_over",
    )(dx, o, p)
    return dx, jnp.transpose(o1, (1, 0, 2)), jnp.transpose(o2, (1, 0, 2)), p


def shards(ndp, nb, x, w1, w2, pw, cot):
    L, px, C = x.shape
    Q = px // 4
    scale = 1.0 / math.sqrt(L * nb * px * ndp)
    if nb == 2 and ndp >= 4 and (C // ndp) % 16 == 0 and L >= HX:
        return hand_over(*step_pass(scale, ndp, x, cot, w1, w2, pw))
    up = [(i, i + 1) for i in range(nb - 1)]
    down = [(j, i) for i, j in up]

    def edges(x_part, c_part, pairs):
        both = jnp.concatenate([x_part.reshape(HX * px, C), c_part.reshape(HC * Q, C)], axis=0)
        both = lax.ppermute(both, "band", pairs)
        return both[:HX * px].reshape(HX, px, C), both[HX * px:].reshape(HC, Q, C)

    xlo, clo = edges(x[L - HX:], cot[L - HC:], up)
    xhi, chi = edges(x[:HX], cot[:HC], down)
    dx, g, gp = local_pass(nb, x, xlo, xhi, cot, clo, chi, w1, w2, pw)
    kept = lax.psum_scatter(g.astype(F32), "dp", scatter_dimension=1, tiled=True)
    kept = (lax.psum(kept, "band") * scale).reshape(2, C // ndp, 3, C)
    o1, o2 = kept[0], kept[1]
    op = lax.psum(gp, ("dp", "band")) * scale
    return dx, o1, o2, op


def solution(mesh):
    placed = (P("band", "dp", None), P(), P(), P(), P("band", "dp", None))
    return jax.shard_map(
        functools.partial(shards, mesh.shape["dp"], mesh.shape["band"]),
        mesh=mesh,
        in_specs=placed,
        out_specs=(P("band", "dp", None), P("dp", None, None), P("dp", None, None), P()),
        check_vma=False,
    )
```

profile of v0, /device:TPU:0, one launch (start us, length us, event | category | flops | bytes accessed | tf_op | source)
XLA Modules:
  0.0 47.0 jit_solution(10748723766202222571)
XLA Ops:
  0.6 41.6 %step_pass.1 = (bf16[112,64,256]{2,1,0:T(8,128)(2,1)}, f32[2,3,16,256]{3,2,1,0:T(8,128)}, f32[4,256]{1,0:T(4,128)}) custom-call(bf16[112,64,256]{2,1,0:T(8,128)(2,1)} %x_hbm.1, bf16[112,16,256]{2,1,0:T(8,128)(2,1)} %cot_hbm.1, bf16[3,256,256]{2,1,0:T(8,128)(2,1)} %w1_ref.1, bf16[3,256,256]{2,1,0:T(8,128)(2,1)} %w2_ref.1, f32[4,256]{1,0:T(4,128)} %pw_ref.1), custom_call_target="tpu_custom_call" | custom-call | tf_op jit(solution)/shard_map/step_pass/pallas_call | solution.py:504
  42.3 4.8 %hand_over.1 = (bf16[112,64,256]{2,1,0:T(8,128)(2,1)}, f32[3,16,256]{2,1,0:T(8,128)}, f32[3,16,256]{2,1,0:T(8,128)}, f32[4,256]{1,0:T(4,128)}) custom-call(bf16[112,64,256]{2,1,0:T(8,128)(2,1)} %get-tuple-element.11.dx_hbm, f32[2,3,16,256]{3,2,1,0:T(8,128)} %get-tuple-element.12.o_ref, f32[4,256]{1,0:T(4,128)} %get-tuple-element.13.p_ref), custom_call_target="tpu_custom_call" | custom-call | tf_op jit(solution)/shard_map/hand_over/pallas_call | solution.py:563
where the time goes:
time: 47.2 us; the launch traced here: 47 us
  Pallas kernels  46.4 us (98%)
  between operations  0.64 us (1%)
    pallas_call x1, Pallas kernels, step_pass(): pl.pallas_call(functools.partial(step_kernel, scale, lo_n, hi_n), out_sha...  41.6 us
    pallas_call x1, Pallas kernels, hand_over(): pl.pallas_call(functools.partial(hand_over_kernel, n), out_shape=(jax.Sha...  4.79 us

commit v1 on v0

--- a/solution.py
+++ b/solution.py
@@ -299,17 +299,53 @@
     )(x, xlo, xhi, cot, clo, chi, w1, w2, pw)
 
 
+def blocks(n, count):
+    size = -(-n // count)
+    return size, [min(i * size, n - size) for i in range(count)]
+
+
+def inner_first(starts, size, n, rim):
+    inner = [s for s in starts if s >= rim and s + size <= n - rim]
+    outer = [s for s in starts if s not in inner]
+    return inner, sorted(outer, reverse=True)
+
+
+def fresh(starts, size, taps, low, high):
+    seen, pieces = set(), []
+    for s in starts:
+        rows = [r for r in range(max(s, low), min(s + size + taps, high)) if r not in seen]
+        seen.update(rows)
+        runs = []
+        for r in rows:
+            if runs and runs[-1][0] + runs[-1][1] == r:
+                runs[-1][1] += 1
+            else:
+                runs.append([r, 1])
+        pieces.append([tuple(run) for run in runs])
+    rest = [r for r in range(low, high) if r not in seen]
+    assert not rest
+    return pieces
+
+
+def first_plan(L):
+    n1 = L + 2 * HZ
+    size, starts = blocks(n1, min(6, n1))
+    inner, outer = inner_first(starts, size, n1, HZ)
+    order = inner + outer
+    return n1, size, order, len(inner), fresh(order, size, 2 * D1, HX, HX + L)
+
+
 def step_kernel(
     scale, lo_n, hi_n,
-    x_hbm, cot_hbm, w1_ref, w2_ref, pw_ref,
-    dx_hbm, o_ref, op_ref,
-    xe, ce, z1e, dh2e, dh1e, u_s, s_s, hs, hs_b, w1t, w2t, acc1, acc2, gpa, sems,
-    gb, r0, s0, r1, s1, r2, fin, rf, p0, p1, p2, q0, hsend, hrecv, ssem, rsem, dxv, dxsem,
+    x_hbm, cot_hbm, w1_hbm, w2_hbm, pw_ref,
+    dx_ref, o_ref, op_ref,
+    xe, ce, z1e, dh2e, dh1e, dt, u_s, s_s, hs_a, hs_b, h2_a, h2_b, dz_a, dz_b,
+    w1, w2, w1t, w2t, gpa, xsem, sems,
+    big, tap, p0, p1, p2, q0, hsend, hrecv, ssem, rsem, spare,
 ):
     L, px, C = x_hbm.shape
     Q = px // 4
-    W = 3 * C
-    half = W // 2
+    H = C // 2
     R = C // (lo_n * hi_n)
     dp = lax.axis_index("dp")
     core = lax.axis_index("band")
@@ -317,23 +353,36 @@
     lo, hi = lax.rem(dp, lo_n), dp // lo_n
     planes = [hi * lo_n + lax.rem(lo + m, lo_n) for m in range(1, lo_n)]
     lines = [lax.rem(hi + m, hi_n) * lo_n + lo for m in range(1, hi_n)]
-    order = [lax.rem(lo + m, lo_n) for m in list(range(1, lo_n)) + [0]]
     partner = (dp, other)
 
     barrier = pltpu.get_barrier_semaphore()
-    targets = [partner] + [(d, core) for d in planes + lines]
+    targets = [partner] + [(d, core) for d in planes] + [(d, c) for d in lines for c in (core, other)]
     for t in targets:
         pl.semaphore_signal(barrier, inc=1, device_id=t, device_id_type=MESH)
 
-    copies = copy_in([(x_hbm, xe.at[pl.ds(HX, L)]), (cot_hbm, ce.at[pl.ds(HC, L)])], sems)
-    turn_weights(w1_ref, w2_ref, w1t, w2t)
+    n1, b1, order1, inner1, pieces = first_plan(L)
+    first = pltpu.make_async_copy(w1_hbm, w1, sems.at[0])
+    first.start()
+    loads, at = [], 0
+    for runs in pieces:
+        mine = []
+        for r, n in runs:
+            c = pltpu.make_async_copy(x_hbm.at[pl.ds(r - HX, n)], xe.at[pl.ds(r, n)], xsem.at[at])
+            c.start()
+            mine.append(c)
+            at += 1
+        loads.append(mine)
+    second = [pltpu.make_async_copy(w2_hbm, w2, sems.at[1]),
+              pltpu.make_async_copy(cot_hbm, ce.at[pl.ds(HC, L)], sems.at[2])]
+    for c in second:
+        c.start()
     xpad = jnp.where(core == 0, 0, HX + L)
     cpad = jnp.where(core == 0, 0, HC + L)
     xe[pl.ds(xpad, HX)] = jnp.zeros((HX, px, C), BF16)
     ce[pl.ds(cpad, HC)] = jnp.zeros((HC, Q, C), BF16)
-    for c in copies:
-        c.wait()
+    gpa[...] = jnp.zeros_like(gpa)
     pw = pw_ref[...]
+    pwb = pw.astype(BF16)
 
     def halos():
         return [
@@ -346,48 +395,13 @@
             for i, (src, dst, w) in enumerate([(x_hbm, xe, HX), (cot_hbm, ce, HC)])
         ]
 
-    def early():
-        pl.semaphore_wait(barrier, len(targets))
-        for c in halos():
-            c.start()
-
-    def late():
-        for c in halos():
-            c.wait()
-
     def link(i, src, dst, target):
         return pltpu.make_async_remote_copy(
             src_ref=src, dst_ref=dst, send_sem=ssem.at[i], recv_sem=rsem.at[i],
             device_id=target, device_id_type=MESH,
         )
 
-    per = lo_n + (lo_n - 1) + (hi_n - 1) + 1
-
-    def across(q):
-        return [link(q * per + m, gb.at[q, other, :, order[m]], r0.at[q, order[m]], partner)
-                for m in range(lo_n)]
-
-    def plane(q):
-        return [link(q * per + lo_n + m, s0.at[q, m], r1.at[q, m], (planes[m], core))
-                for m in range(lo_n - 1)]
-
-    def line(q):
-        return [link(q * per + 2 * lo_n - 1 + m, s1.at[q, lax.rem(hi + m + 1, hi_n)], r2.at[q, m],
-                     (lines[m], core)) for m in range(hi_n - 1)]
-
-    def ends(q):
-        return [link(q * per + per - 1, fin.at[q], rf.at[q], partner)]
-
-    def pairs_p():
-        return [link(2 * per, q0.at[0], p0, partner)]
-
-    def plane_p():
-        return [link(2 * per + 1 + m, q0.at[1], p1.at[lo], (planes[m], core))
-                for m in range(lo_n - 1)]
-
-    def line_p():
-        return [link(2 * per + lo_n + m, q0.at[2], p2.at[hi], (lines[m], core))
-                for m in range(hi_n - 1)]
+    per = 1 + (lo_n - 1) + 2 * (hi_n - 1) + 1
 
     def start(cs):
         for c in cs:
@@ -397,43 +411,76 @@
         for c in cs:
             c.wait_recv()
 
-    def step_a(q, acc):
-        for h in range(2):
-            gb[q, h] = acc[:, h * half:(h + 1) * half].astype(BF16).reshape(hi_n, lo_n, R, half)
-        start(across(q))
-
-    def step_b(q):
-        into, out = across(q), plane(q)
-        for m in range(lo_n):
-            into[m].wait_recv()
-            if m == lo_n - 1:
-                break
-            total = gb[q, core, :, order[m]].astype(F32) + r0[q, order[m]].astype(F32)
-            s0[q, m] = total.astype(BF16)
-            out[m].start()
-
-    def step_c(q):
-        arrived(plane(q))
-        own = gb[q, core, :, lo].astype(F32) + r0[q, lo].astype(F32)
-        for m in range(lo_n - 1):
-            own = own + r1[q, m].astype(F32)
-        s1[q] = own.astype(BF16)
-        start(line(q))
-
-    def step_d(q):
-        arrived(line(q))
-        mine = s1[q, hi].astype(F32)
-        for m in range(hi_n - 1):
-            mine = mine + r2[q, m].astype(F32)
-        fin[q] = mine * scale
-        start(ends(q))
-
-    def step_e(q):
-        arrived(ends(q))
-        a, b = fin[q], rf[q]
-        row = jnp.concatenate([jnp.where(core == 0, a, b), jnp.where(core == 0, b, a)], axis=-1)
-        for k in range(3):
-            o_ref[q, k] = row[:, k * C:(k + 1) * C]
+    def reducer(slot, refs):
+        gb, r0, s0, r1, s1, r2 = refs
+        base = slot * per
+
+        def across():
+            return [link(base, gb.at[other], r0, partner)]
+
+        def plane():
+            return [link(base + 1 + m, s0.at[m], r1.at[m], (planes[m], core))
+                    for m in range(lo_n - 1)]
+
+        def line():
+            out = []
+            for m in sorted(range(hi_n - 1), key=lambda m: abs(m + 1 - hi_n / 2)):
+                src = s1.at[lax.rem(hi + m + 1, hi_n)]
+                for k, c in enumerate((core, other)):
+                    out.append(link(base + lo_n + 2 * m + k, src, r2.at[k, m], (lines[m], c)))
+            out.append(link(base + per - 1, s1.at[hi], r2.at[1, hi_n - 1], partner))
+            return out
+
+        def step_a(parts):
+            for h in range(2):
+                for k, part in enumerate(parts):
+                    rows = part[:, h * H:(h + 1) * H].astype(BF16).reshape(hi_n, lo_n, R, H)
+                    for l in range(lo_n):
+                        gb[h, l, :, :, k * H:(k + 1) * H] = rows[:, l]
+            start(across())
+
+        def step_b():
+            arrived(across())
+            out = plane()
+            for m in range(lo_n - 1):
+                at = lax.rem(lo + m + 1, lo_n)
+                s0[m] = (gb[core, at].astype(F32) + r0[at].astype(F32)).astype(BF16)
+                out[m].start()
+
+        def step_c():
+            arrived(plane())
+            own = gb[core, lo].astype(F32) + r0[lo].astype(F32)
+            for m in range(lo_n - 1):
+                own = own + r1[m].astype(F32)
+            s1[...] = own.astype(BF16)
+            start(line())
+
+        def step_d(put):
+            arrived(line())
+            mine = s1[hi].astype(F32)
+            theirs = r2[1, hi_n - 1].astype(F32)
+            for m in range(hi_n - 1):
+                mine = mine + r2[0, m].astype(F32)
+                theirs = theirs + r2[1, m].astype(F32)
+            a = jnp.where(core == 0, mine, theirs) * scale
+            b = jnp.where(core == 0, theirs, mine) * scale
+            for k in range(a.shape[-1] // H):
+                put(k, jnp.concatenate([a[:, k * H:(k + 1) * H], b[:, k * H:(k + 1) * H]], axis=-1))
+
+        return step_a, step_b, step_c, step_d, lambda: across() + plane() + line()
+
+    second_sum = reducer(0, big)
+    tap_sums = [reducer(1 + k, [r.at[k] for r in tap]) for k in range(3)]
+    pbase = 4 * per
+
+    def pairs_p():
+        return [link(pbase, q0.at[0], p0, partner)]
+
+    def plane_p():
+        return [link(pbase + 1 + m, q0.at[1], p1.at[lo], (planes[m], core)) for m in range(lo_n - 1)]
+
+    def line_p():
+        return [link(pbase + lo_n + m, q0.at[2], p2.at[hi], (lines[m], core)) for m in range(hi_n - 1)]
 
     def patch_a():
         q0[0] = jnp.sum(gpa[...], axis=1)
@@ -456,118 +503,303 @@
         arrived(line_p())
         op_ref[...] = jnp.sum(p2[...], axis=0) * scale
 
-    first_layer(core, 2, early, late, xe, w1_ref, pw, hs, hs_b, u_s, s_s, z1e)
-    second_layer(z1e, ce, w2_ref, dh2e, acc2)
-    step_a(1, acc2[...])
-    first_delta(core, 2, dh2e, w2t, pw, u_s, s_s, hs, gpa, dh1e, xe, acc1)
-    step_a(0, acc1[...])
+    def mix(i, hs):
+        s = order1[i]
+        for c in loads[i]:
+            c.wait()
+        h = dot(stacked(xe, [s, s + D1, s + 2 * D1], b1), w1[...].reshape(3 * C, C))
+        for t in range(2):
+            hs[t, :b1 * px] = h[:, t * H:(t + 1) * H]
+
+    def activate(i, hs):
+        s = order1[i]
+        g = divisor(b1, 8)
+        for r in range(0, b1, g):
+            for t in range(2):
+                cols = slice(t * H, (t + 1) * H)
+                z = None
+                for j in range(4):
+                    v = hs[t, pl.ds(r * px + j, g * Q, stride=4), :].astype(BF16)
+                    u, sl = gelu_terms(v)
+                    u_s[j, s + r:s + r + g, :, cols] = u.astype(u_s.dtype).reshape(g, Q, H)
+                    s_s[j, s + r:s + r + g, :, cols] = sl.astype(s_s.dtype).reshape(g, Q, H)
+                    term = (u * pwb[j:j + 1, cols]).astype(F32)
+                    z = term if z is None else z + term
+                z1e[s + r:s + r + g, :, cols] = z.reshape(g, Q, H).astype(BF16)
+
+    n2 = L + 2 * HC
+    b2, starts2 = blocks(n2, min(3, n2))
+    order2 = sum(inner_first(starts2, b2, n2, HC), [])
+
+    def mix2(i, h2):
+        s = order2[i]
+        h2[...] = dot(stacked(z1e, [s, s + D2, s + 2 * D2], b2), w2[...].reshape(3 * C, C))
+
+    def activate2(i, h2):
+        s = order2[i]
+        g = divisor(b2, 8)
+        for r in range(0, b2, g):
+            sl = gelu_terms(h2[r * Q:(r + g) * Q, :])[1]
+            d = ce[s + r:s + r + g].reshape(g * Q, C).astype(F32) * sl
+            dh2e[s + r:s + r + g] = d.astype(BF16).reshape(g, Q, C)
+
+    n3 = L + 2
+    b3, order3 = blocks(n3, min(3, n3))
+
+    def mix3(i, dz):
+        s = order3[i] + HC - 1
+        dz[...] = dot(stacked(dh2e, [s + D2, s, s - D2], b3), w2t[...])
+
+    def delta(i, dz, hs):
+        s = order3[i]
+        done = 0 if i == 0 else order3[i - 1] + b3
+        g = divisor(b3, 8)
+        for r in range(0, b3, g):
+            own = [b for b in range(s + r, s + r + g) if 1 <= b <= L and b >= done]
+            for t in range(2):
+                cols = slice(t * H, (t + 1) * H)
+                d = dz[r * Q:(r + g) * Q, cols].astype(BF16)
+                for j in range(4):
+                    where = slice(s + r + HZ - 1, s + r + g + HZ - 1)
+                    u = u_s[j, where, :, cols].reshape(g * Q, H)
+                    sl = s_s[j, where, :, cols].reshape(g * Q, H)
+                    hs[t, pl.ds(r * px + j, g * Q, stride=4), :] = (
+                        d * pwb[j:j + 1, cols] * sl).astype(F32)
+                    if own:
+                        a, b = (own[0] - s - r) * Q, (own[-1] + 1 - s - r) * Q
+                        m = (d[a:b] * u[a:b]).reshape(len(own), Q, H)
+                        part = m[0]
+                        for k in range(1, len(own)):
+                            part = part + m[k]
+                        gpa[j, :, cols] += part.astype(F32)
+            for t in range(2):
+                cols = slice(t * H, (t + 1) * H)
+                dh1e[s + r:s + r + g, :, cols] = (
+                    hs[t, r * px:(r + g) * px].astype(BF16).reshape(g, px, H))
+
+    bt = max(b for b in range(1, min(L, 16) + 1) if L % b == 0 and b * px % 128 == 0)
+
+    def turn(upto):
+        while turned[0] < L // bt and (turned[0] + 1) * bt + 1 <= upto:
+            i = turned[0]
+            dt[:, i * bt * px:(i + 1) * bt * px] = dh1e[1 + i * bt:1 + (i + 1) * bt].reshape(bt * px, C).T
+            turned[0] += 1
+
+    turned = [0]
+
+    def first_gradient(k):
+        x = xe[pl.ds(HX + (k - 1) * D1, L)].reshape(L * px, C)
+        tap_sums[k][0]([dot(dt[...], x)])
+
+    def input_gradient_of(b, n):
+        g = dot(stacked(dh1e, [b + 1 + D1, b + 1, b + 1 - D1], n), w1t[...])
+        dx_ref[pl.ds(b, n)] = g.astype(BF16).reshape(n, px, C)
+
+    first.wait()
+    steps = len(order1)
+    hs = [hs_a, hs_b]
+    for i in range(steps + 1):
+        if i < steps:
+            if i == inner1:
+                for c in halos():
+                    c.wait()
+            mix(i, hs[i % 2])
+        if i == 0:
+            pl.semaphore_wait(barrier, len(targets))
+            for c in halos():
+                c.start()
+        if i == 2:
+            for c in second:
+                c.wait()
+            turn_weights(w1, w2, w1t, w2t)
+        if i:
+            activate(i - 1, hs[(i - 1) % 2])
+
+    @pl.when(core == 0)
+    def _():
+        z1e[pl.ds(0, HZ)] = jnp.zeros((HZ, Q, C), BF16)
+
+    @pl.when(core == 1)
+    def _():
+        z1e[pl.ds(HZ + L, HZ)] = jnp.zeros((HZ, Q, C), BF16)
+
+    h2 = [h2_a, h2_b]
+    for i in range(len(order2) + 1):
+        if i < len(order2):
+            mix2(i, h2[i % 2])
+        if i:
+            activate2(i - 1, h2[(i - 1) % 2])
+
+    dz = [dz_a, dz_b]
+    mix3(0, dz[0])
+    d2 = dh2e[pl.ds(HC, L)].reshape(L * Q, C)
+    acc2 = dot_rows(d2, stacked(z1e, [HZ - D2, HZ, HZ + D2], L))
+    second_sum[0]([acc2[:, k * C:(k + 1) * C] for k in range(3)])
+    count = len(order3)
+    for i in range(count):
+        if i + 1 < count:
+            mix3(i + 1, dz[(i + 1) % 2])
+        delta(i, dz[i % 2], hs[i % 2])
+        if i + 1 < count:
+            turn(order3[i] + b3)
+        if i == count - 2:
+            second_sum[1]()
+
     patch_a()
-    step_b(1)
-
-    def hook_one():
-        patch_b()
-
-    def hook_two():
-        step_b(0)
-
-    def hook_three():
-        step_c(1)
-        patch_c()
-
-    def finish(bands):
-        pltpu.make_async_copy(dxv.at[bands], dx_hbm.at[bands], dxsem.at[0]).start()
-
-    input_gradient(dh1e, w1t, dxv, [(3, hook_two), (4, hook_one), (11, hook_three)], finish)
-    step_c(0)
-    step_d(1)
-    step_e(1)
+
+    @pl.when(core == 0)
+    def _():
+        dh1e[0] = jnp.zeros((px, C), BF16)
+
+    @pl.when(core == 1)
+    def _():
+        dh1e[L + 1] = jnp.zeros((px, C), BF16)
+
+    turn(n3)
+    first_gradient(0)
+    first_gradient(1)
+    patch_b()
+    first_gradient(2)
+    tap_sums[0][1]()
+    pieces4 = 4 if L % 4 == 0 else 1
+    n = L // pieces4
+    after = [
+        [tap_sums[1][1]],
+        [tap_sums[2][1]],
+        [second_sum[2], patch_c],
+        [],
+    ]
+
+    def put2(k, row):
+        o_ref[1, k] = row
+
+    def put1(tap_index):
+        def put(k, row):
+            o_ref[0, tap_index] = row
+        return put
+
+    for i in range(pieces4):
+        input_gradient_of(i * n, n)
+        for hook in (after[i] if pieces4 == 4 else sum(after, [])):
+            hook()
+    tap_sums[0][2]()
+    tap_sums[1][2]()
+    tap_sums[2][2]()
     patch_d()
-    step_d(0)
-    step_e(0)
-    for q in range(2):
-        for c in across(q) + plane(q) + line(q) + ends(q):
+    second_sum[3](put2)
+    for k in range(3):
+        tap_sums[k][3](put1(k))
+    for part in [second_sum] + tap_sums:
+        for c in part[4]():
             c.wait_send()
     for c in pairs_p() + plane_p() + line_p():
         c.wait_send()
-    pltpu.make_async_copy(dxv, dx_hbm, dxsem.at[0]).wait()
 
 
 def step_pass(scale, ndp, x, cot, w1, w2, pw):
     L, px, C = x.shape
+    Q = px // 4
+    H = C // 2
     R = C // ndp
-    half = 3 * C // 2
     lo_n = divisor(ndp, math.isqrt(ndp))
     hi_n = ndp // lo_n
-    n = 2 * (2 * lo_n + hi_n - 1) + lo_n + hi_n - 1
-    any_spec = pl.BlockSpec(memory_space=pl.ANY)
+    n = 4 * (lo_n + 2 * (hi_n - 1) + 1) + lo_n + hi_n - 1
+    hbm = pl.BlockSpec(memory_space=pltpu.HBM)
     vm = pl.BlockSpec(memory_space=pltpu.VMEM)
+    _, b1, _, _, pieces = first_plan(L)
+    b2 = blocks(L + 2 * HC, 3)[0]
+    b3 = blocks(L + 2, 3)[0]
+    wide = max(b1, b3)
+
+    def sums(lead, w):
+        return [
+            pltpu.VMEM(lead + (2, lo_n, hi_n, R, w), BF16),
+            pltpu.VMEM(lead + (lo_n, hi_n, R, w), BF16),
+            pltpu.VMEM(lead + (lo_n - 1, hi_n, R, w), BF16),
+            pltpu.VMEM(lead + (lo_n - 1, hi_n, R, w), BF16),
+            pltpu.VMEM(lead + (hi_n, R, w), BF16),
+            pltpu.VMEM(lead + (2, hi_n, R, w), BF16),
+        ]
+
+    limit = 67043328 - (L * px * C * 2 + (1 << 18))
+    scratch = [
+        pltpu.VMEM((L + 2 * HX, px, C), BF16),
+        pltpu.VMEM((L + 2 * HC, Q, C), BF16),
+        pltpu.VMEM((L + 2 * HZ, Q, C), BF16),
+        pltpu.VMEM((L + 2 * HC, Q, C), BF16),
+        pltpu.VMEM((L + 2, px, C), BF16),
+        pltpu.VMEM((C, L * px), BF16),
+        pltpu.VMEM((4, L + 2 * HZ, Q, C), BF16),
+        pltpu.VMEM((4, L + 2 * HZ, Q, C), BF16),
+        pltpu.VMEM((2, wide * px, H), F32),
+        pltpu.VMEM((2, wide * px, H), F32),
+        pltpu.VMEM((b2 * Q, C), F32),
+        pltpu.VMEM((b2 * Q, C), F32),
+        pltpu.VMEM((b3 * Q, C), F32),
+        pltpu.VMEM((b3 * Q, C), F32),
+        pltpu.VMEM((3, C, C), BF16),
+        pltpu.VMEM((3, C, C), BF16),
+        pltpu.VMEM((3 * C, C), BF16),
+        pltpu.VMEM((3 * C, C), BF16),
+        pltpu.VMEM((4, Q, C), F32),
+        pltpu.SemaphoreType.DMA((sum(len(p) for p in pieces),)),
+        pltpu.SemaphoreType.DMA((3,)),
+        sums((), 3 * H),
+        sums((3,), H),
+        pltpu.VMEM((4, C), F32),
+        pltpu.VMEM((lo_n, 4, C), F32),
+        pltpu.VMEM((hi_n, 4, C), F32),
+        pltpu.VMEM((3, 4, C), F32),
+        pltpu.SemaphoreType.DMA((2,)),
+        pltpu.SemaphoreType.DMA((2,)),
+        pltpu.SemaphoreType.DMA((n,)),
+        pltpu.SemaphoreType.DMA((n,)),
+    ]
+    used = sum(math.prod(r.shape) * jnp.dtype(r.dtype).itemsize
+               for r in jax.tree.leaves(scratch) if r.memory_space == pltpu.VMEM)
+    spare = max((limit - used - (1 << 20)) // (8 * 128 * 4), 1) * 128
     return pl.pallas_call(
         functools.partial(step_kernel, scale, lo_n, hi_n),
         out_shape=(
-            jax.ShapeDtypeStruct((L, px, C), BF16),
-            jax.ShapeDtypeStruct((2, 3, R, C), F32),
-            jax.ShapeDtypeStruct((4, C), F32),
+            pltpu.VMEM((L, px, C), BF16),
+            pltpu.VMEM((2, 3, R, C), F32),
+            pltpu.VMEM((4, C), F32),
         ),
-        in_specs=[any_spec] * 2 + [vm] * 3,
-        out_specs=[any_spec, vm, vm],
-        scratch_shapes=local_scratch(L, px, C) + [
-            pltpu.VMEM((2, 2, hi_n, lo_n, R, half), BF16),
-            pltpu.VMEM((2, lo_n, hi_n, R, half), BF16),
-            pltpu.VMEM((2, lo_n - 1, hi_n, R, half), BF16),
-            pltpu.VMEM((2, lo_n - 1, hi_n, R, half), BF16),
-            pltpu.VMEM((2, hi_n, R, half), BF16),
-            pltpu.VMEM((2, hi_n - 1, R, half), BF16),
-            pltpu.VMEM((2, R, half), F32),
-            pltpu.VMEM((2, R, half), F32),
-            pltpu.VMEM((4, C), F32),
-            pltpu.VMEM((lo_n, 4, C), F32),
-            pltpu.VMEM((hi_n, 4, C), F32),
-            pltpu.VMEM((3, 4, C), F32),
-            pltpu.SemaphoreType.DMA((2,)),
-            pltpu.SemaphoreType.DMA((2,)),
-            pltpu.SemaphoreType.DMA((n,)),
-            pltpu.SemaphoreType.DMA((n,)),
-            pltpu.VMEM((L, px, C), BF16),
-            pltpu.SemaphoreType.DMA((1,)),
-        ],
+        in_specs=[hbm] * 4 + [vm],
+        out_specs=[vm, vm, vm],
+        scratch_shapes=scratch + [pltpu.VMEM((8, spare), F32)],
         compiler_params=pltpu.CompilerParams(
-            collective_id=0, has_side_effects=True, vmem_limit_bytes=60 * 1024 * 1024
+            collective_id=0, has_side_effects=True, vmem_limit_bytes=limit
         ),
         name="step_pass",
     )(x, cot, w1, w2, pw)
 
 
-def hand_over_kernel(n, dx_hbm, o_ref, p_ref, dx_out, o1_out, o2_out, p_out, buf, isem, osem):
-    step = dx_hbm.shape[0] // n
-    into = [pltpu.make_async_copy(dx_hbm.at[pl.ds(i * step, step)], buf.at[pl.ds(i * step, step)],
-                                  isem.at[i]) for i in range(n)]
-    out = [pltpu.make_async_copy(buf.at[pl.ds(i * step, step)], dx_out.at[pl.ds(i * step, step)],
-                                 osem.at[i]) for i in range(n)]
-    for c in into:
+def hand_over_kernel(n, dx_ref, o_ref, p_ref, dx_out, o1_out, o2_out, p_out, sem):
+    step = dx_ref.shape[0] // n
+    out = [pltpu.make_async_copy(dx_ref.at[pl.ds(i * step, step)], dx_out.at[pl.ds(i * step, step)],
+                                 sem.at[i]) for i in range(n)]
+    for c in out:
         c.start()
     o1_out[...] = o_ref[0]
     o2_out[...] = o_ref[1]
     p_out[...] = p_ref[...]
-    for a, b in zip(into, out):
-        a.wait()
-        b.start()
-    for b in out:
-        b.wait()
+    for c in out:
+        c.wait()
 
 
 def hand_over(dx, o, p):
-    n = divisor(dx.shape[0], 14)
+    n = divisor(dx.shape[0], 4)
     vm = pl.BlockSpec(memory_space=pltpu.VMEM)
-    any_spec = pl.BlockSpec(memory_space=pl.ANY)
     one = jax.ShapeDtypeStruct(o.shape[1:], F32)
     dx, o1, o2, p = pl.pallas_call(
         functools.partial(hand_over_kernel, n),
         out_shape=(jax.ShapeDtypeStruct(dx.shape, dx.dtype), one, one,
                    jax.ShapeDtypeStruct(p.shape, F32)),
-        in_specs=[any_spec, vm, vm],
-        out_specs=[any_spec, vm, vm, vm],
-        scratch_shapes=[pltpu.VMEM(dx.shape, dx.dtype), pltpu.SemaphoreType.DMA((n,)),
-                        pltpu.SemaphoreType.DMA((n,))],
+        in_specs=[vm, vm, vm],
+        out_specs=[pl.BlockSpec(memory_space=pltpu.HBM), vm, vm, vm],
+        scratch_shapes=[pltpu.SemaphoreType.DMA((n,))],
+        compiler_params=pltpu.CompilerParams(vmem_limit_bytes=16 * 1024 * 1024),
         name="hand_over",
     )(dx, o, p)
     return dx, jnp.transpose(o1, (1, 0, 2)), jnp.transpose(o2, (1, 0, 2)), p
@@ -577,7 +809,7 @@
     L, px, C = x.shape
     Q = px // 4
     scale = 1.0 / math.sqrt(L * nb * px * ndp)
-    if nb == 2 and ndp >= 4 and (C // ndp) % 16 == 0 and L >= HX:
+    if nb == 2 and ndp >= 4 and (C // ndp) % 16 == 0 and C % 256 == 0 and L >= 48 and L * px % 128 == 0:
         return hand_over(*step_pass(scale, ndp, x, cot, w1, w2, pw))
     up = [(i, i + 1) for i in range(nb - 1)]
     down = [(j, i) for i, j in up]

time: 47.2 us -> 40.9 us (0.87)
  Pallas kernels: 46.4 us -> 39.9 us
    pallas_call x1, Pallas kernels: 41.6 us -> 37.4 us  [step_pass(): pl.pallas_call(functools.partial(step_kernel, scale, lo_n, hi_n), out_sha...]
    pallas_call x1, Pallas kernels: 4.79 us -> 2.5 us  [hand_over(): pl.pallas_call(functools.partial(hand_over_kernel, n), out_shape=(jax.Sha...]
where the time goes in v1:
time: 40.9 us; the launch traced here: 40.7 us
  Pallas kernels  39.9 us (98%)
  between operations  0.8 us (2%)
    pallas_call x1, Pallas kernels, step_pass(): pl.pallas_call(functools.partial(step_kernel, scale, lo_n, hi_n), out_sha...  37.4 us
    pallas_call x1, Pallas kernels, hand_over(): pl.pallas_call(functools.partial(hand_over_kernel, n), out_shape=(jax.Sha...  2.5 us

profile of v1, /device:TPU:0, one launch (start us, length us, event | category | flops | bytes accessed | tf_op | source)
XLA Modules:
  0.0 40.7 jit_solution(10610827588690374348)
XLA Ops:
  0.6 37.4 %step_pass.1 = (bf16[112,64,256]{2,1,0:T(8,128)(2,1)S(1)}, f32[2,3,16,256]{3,2,1,0:T(8,128)S(1)}, f32[4,256]{1,0:T(4,128)S(1)}) custom-call(bf16[112,64,256]{2,1,0:T(8,128)(2,1)} %x_hbm.1, bf16[112,16,256]{2,1,0:T(8,128)(2,1)} %cot_hbm.1, bf16[3,256,256]{2,1,0:T(8,128)(2,1)} %w1_hbm.1, bf16[3,256,256]{2,1,0:T(8,128)(2,1)} %w2_hbm.1, f32[4,256]{1,0:T(4,128)} %pw_ref.1), custom_call_target="tpu_custom_call" | custom-call | tf_op jit(solution)/shard_map/step_pass/pallas_call | solution.py:761
  38.0 2.5 %hand_over.1 = (bf16[112,64,256]{2,1,0:T(8,128)(2,1)}, f32[3,16,256]{2,1,0:T(8,128)}, f32[3,16,256]{2,1,0:T(8,128)}, f32[4,256]{1,0:T(4,128)}) custom-call(bf16[112,64,256]{2,1,0:T(8,128)(2,1)S(1)} %get-tuple-element.11.dx_ref, f32[2,3,16,256]{3,2,1,0:T(8,128)S(1)} %get-tuple-element.12.o_ref, f32[4,256]{1,0:T(4,128)S(1)} %get-tuple-element.13.p_ref), custom_call_target="tpu_custom_call" | custom-call | tf_op jit(solution)/shard_map/hand_over/pallas_call | solution.py:795

commit v2 on v1

--- a/solution.py
+++ b/solution.py
@@ -341,7 +341,7 @@
     dx_ref, o_ref, op_ref,
     xe, ce, z1e, dh2e, dh1e, dt, u_s, s_s, hs_a, hs_b, h2_a, h2_b, dz_a, dz_b,
     w1, w2, w1t, w2t, gpa, xsem, sems,
-    big, tap, p0, p1, p2, q0, hsend, hrecv, ssem, rsem, spare,
+    big, tap, acc1, p0, p1, p2, q0, hsend, hrecv, ssem, rsem, spare,
 ):
     L, px, C = x_hbm.shape
     Q = px // 4
@@ -470,8 +470,8 @@
         return step_a, step_b, step_c, step_d, lambda: across() + plane() + line()
 
     second_sum = reducer(0, big)
-    tap_sums = [reducer(1 + k, [r.at[k] for r in tap]) for k in range(3)]
-    pbase = 4 * per
+    first_sum = reducer(1, tap)
+    pbase = 2 * per
 
     def pairs_p():
         return [link(pbase, q0.at[0], p0, partner)]
@@ -544,7 +544,7 @@
             dh2e[s + r:s + r + g] = d.astype(BF16).reshape(g, Q, C)
 
     n3 = L + 2
-    b3, order3 = blocks(n3, min(3, n3))
+    b3, order3 = blocks(n3, 4)
 
     def mix3(i, dz):
         s = order3[i] + HC - 1
@@ -577,7 +577,8 @@
                 dh1e[s + r:s + r + g, :, cols] = (
                     hs[t, r * px:(r + g) * px].astype(BF16).reshape(g, px, H))
 
-    bt = max(b for b in range(1, min(L, 16) + 1) if L % b == 0 and b * px % 128 == 0)
+    share = L // 4
+    bt = max(b for b in range(1, 17) if share % b == 0 and b * px % 128 == 0)
 
     def turn(upto):
         while turned[0] < L // bt and (turned[0] + 1) * bt + 1 <= upto:
@@ -587,9 +588,15 @@
 
     turned = [0]
 
-    def first_gradient(k):
-        x = xe[pl.ds(HX + (k - 1) * D1, L)].reshape(L * px, C)
-        tap_sums[k][0]([dot(dt[...], x)])
+    def first_gradient(c):
+        x = stacked(xe, [HX + c * share + k * D1 for k in (-1, 0, 1)], share)
+        g = dot(dt[:, c * share * px:(c + 1) * share * px], x)
+        if c == 0:
+            acc1[...] = g
+        elif c < 3:
+            acc1[...] += g
+        else:
+            first_sum[0]([acc1[:, k * C:(k + 1) * C] + g[:, k * C:(k + 1) * C] for k in range(3)])
 
     def input_gradient_of(b, n):
         g = dot(stacked(dh1e, [b + 1 + D1, b + 1, b + 1 - D1], n), w1t[...])
@@ -637,12 +644,12 @@
     second_sum[0]([acc2[:, k * C:(k + 1) * C] for k in range(3)])
     count = len(order3)
     for i in range(count):
+        delta(i, dz[i % 2], hs[i % 2])
         if i + 1 < count:
             mix3(i + 1, dz[(i + 1) % 2])
-        delta(i, dz[i % 2], hs[i % 2])
-        if i + 1 < count:
             turn(order3[i] + b3)
-        if i == count - 2:
+            first_gradient(i)
+        if i == 1:
             second_sum[1]()
 
     patch_a()
@@ -656,44 +663,25 @@
         dh1e[L + 1] = jnp.zeros((px, C), BF16)
 
     turn(n3)
-    first_gradient(0)
-    first_gradient(1)
+    first_gradient(3)
     patch_b()
-    first_gradient(2)
-    tap_sums[0][1]()
-    pieces4 = 4 if L % 4 == 0 else 1
-    n = L // pieces4
-    after = [
-        [tap_sums[1][1]],
-        [tap_sums[2][1]],
-        [second_sum[2], patch_c],
-        [],
-    ]
-
-    def put2(k, row):
-        o_ref[1, k] = row
-
-    def put1(tap_index):
-        def put(k, row):
-            o_ref[0, tap_index] = row
-        return put
-
-    for i in range(pieces4):
-        input_gradient_of(i * n, n)
-        for hook in (after[i] if pieces4 == 4 else sum(after, [])):
+    after = [[], [first_sum[1]], [second_sum[2], patch_c], []]
+
+    def put(q):
+        def row(k, value):
+            o_ref[q, k] = value
+        return row
+
+    for i in range(4):
+        input_gradient_of(i * share, share)
+        for hook in after[i]:
             hook()
-    tap_sums[0][2]()
-    tap_sums[1][2]()
-    tap_sums[2][2]()
+    first_sum[2]()
     patch_d()
-    second_sum[3](put2)
-    for k in range(3):
-        tap_sums[k][3](put1(k))
-    for part in [second_sum] + tap_sums:
-        for c in part[4]():
-            c.wait_send()
-    for c in pairs_p() + plane_p() + line_p():
+    second_sum[3](put(1))
+    for c in second_sum[4]() + pairs_p() + plane_p() + line_p() + first_sum[4]():
         c.wait_send()
+    first_sum[3](put(0))
 
 
 def step_pass(scale, ndp, x, cot, w1, w2, pw):
@@ -703,12 +691,12 @@
     R = C // ndp
     lo_n = divisor(ndp, math.isqrt(ndp))
     hi_n = ndp // lo_n
-    n = 4 * (lo_n + 2 * (hi_n - 1) + 1) + lo_n + hi_n - 1
+    n = 2 * (lo_n + 2 * (hi_n - 1) + 1) + lo_n + hi_n - 1
     hbm = pl.BlockSpec(memory_space=pltpu.HBM)
     vm = pl.BlockSpec(memory_space=pltpu.VMEM)
     _, b1, _, _, pieces = first_plan(L)
     b2 = blocks(L + 2 * HC, 3)[0]
-    b3 = blocks(L + 2, 3)[0]
+    b3 = blocks(L + 2, 4)[0]
     wide = max(b1, b3)
 
     def sums(lead, w):
@@ -745,7 +733,8 @@
         pltpu.SemaphoreType.DMA((sum(len(p) for p in pieces),)),
         pltpu.SemaphoreType.DMA((3,)),
         sums((), 3 * H),
-        sums((3,), H),
+        sums((), 3 * H),
+        pltpu.VMEM((C, 3 * C), F32),
         pltpu.VMEM((4, C), F32),
         pltpu.VMEM((lo_n, 4, C), F32),
         pltpu.VMEM((hi_n, 4, C), F32),
@@ -809,7 +798,7 @@
     L, px, C = x.shape
     Q = px // 4
     scale = 1.0 / math.sqrt(L * nb * px * ndp)
-    if nb == 2 and ndp >= 4 and (C // ndp) % 16 == 0 and C % 256 == 0 and L >= 48 and L * px % 128 == 0:
+    if nb == 2 and ndp >= 4 and (C // ndp) % 16 == 0 and C % 256 == 0 and L >= 48 and L % 8 == 0 and px % 16 == 0:
         return hand_over(*step_pass(scale, ndp, x, cot, w1, w2, pw))
     up = [(i, i + 1) for i in range(nb - 1)]
     down = [(j, i) for i, j in up]

time: 40.9 us -> 37.6 us (0.919)
  Pallas kernels: 39.9 us -> 36.6 us
    pallas_call x1, Pallas kernels: 37.4 us -> 34.1 us  [step_pass(): pl.pallas_call(functools.partial(step_kernel, scale, lo_n, hi_n), out_sha...]
where the time goes in v2:
time: 37.6 us; the launch traced here: 37.4 us
  Pallas kernels  36.6 us (97%)
  between operations  0.8 us (2%)
    pallas_call x1, Pallas kernels, step_pass(): pl.pallas_call(functools.partial(step_kernel, scale, lo_n, hi_n), out_sha...  34.1 us
    pallas_call x1, Pallas kernels, hand_over(): pl.pallas_call(functools.partial(hand_over_kernel, n), out_shape=(jax.Sha...  2.5 us

profile of v2, /device:TPU:0, one launch (start us, length us, event | category | flops | bytes accessed | tf_op | source)
XLA Modules:
  0.0 37.4 jit_solution(5983443176131593443)
XLA Ops:
  0.6 34.1 %step_pass.1 = (bf16[112,64,256]{2,1,0:T(8,128)(2,1)S(1)}, f32[2,3,16,256]{3,2,1,0:T(8,128)S(1)}, f32[4,256]{1,0:T(4,128)S(1)}) custom-call(bf16[112,64,256]{2,1,0:T(8,128)(2,1)} %x_hbm.1, bf16[112,16,256]{2,1,0:T(8,128)(2,1)} %cot_hbm.1, bf16[3,256,256]{2,1,0:T(8,128)(2,1)} %w1_hbm.1, bf16[3,256,256]{2,1,0:T(8,128)(2,1)} %w2_hbm.1, f32[4,256]{1,0:T(4,128)} %pw_ref.1), custom_call_target="tpu_custom_call" | custom-call | tf_op jit(solution)/shard_map/step_pass/pallas_call | solution.py:750
  34.8 2.5 %hand_over.1 = (bf16[112,64,256]{2,1,0:T(8,128)(2,1)}, f32[3,16,256]{2,1,0:T(8,128)}, f32[3,16,256]{2,1,0:T(8,128)}, f32[4,256]{1,0:T(4,128)}) custom-call(bf16[112,64,256]{2,1,0:T(8,128)(2,1)S(1)} %get-tuple-element.11.dx_ref, f32[2,3,16,256]{3,2,1,0:T(8,128)S(1)} %get-tuple-element.12.o_ref, f32[4,256]{1,0:T(4,128)S(1)} %get-tuple-element.13.p_ref), custom_call_target="tpu_custom_call" | custom-call | tf_op jit(solution)/shard_map/hand_over/pallas_call | solution.py:784

commit v3 on v2

--- a/solution.py
+++ b/solution.py
@@ -299,6 +299,10 @@
     )(x, xlo, xhi, cot, clo, chi, w1, w2, pw)
 
 
+def groups(n, most):
+    return [(r, min(most, n - r)) for r in range(0, n, most)]
+
+
 def blocks(n, count):
     size = -(-n // count)
     return size, [min(i * size, n - size) for i in range(count)]
@@ -513,16 +517,15 @@
 
     def activate(i, hs):
         s = order1[i]
-        g = divisor(b1, 8)
-        for r in range(0, b1, g):
+        for r, g in groups(b1, 8):
             for t in range(2):
                 cols = slice(t * H, (t + 1) * H)
                 z = None
                 for j in range(4):
                     v = hs[t, pl.ds(r * px + j, g * Q, stride=4), :].astype(BF16)
                     u, sl = gelu_terms(v)
-                    u_s[j, s + r:s + r + g, :, cols] = u.astype(u_s.dtype).reshape(g, Q, H)
-                    s_s[j, s + r:s + r + g, :, cols] = sl.astype(s_s.dtype).reshape(g, Q, H)
+                    u_s[j, s + r:s + r + g, t] = u.astype(u_s.dtype).reshape(g, Q, H)
+                    s_s[j, s + r:s + r + g, t] = sl.astype(s_s.dtype).reshape(g, Q, H)
                     term = (u * pwb[j:j + 1, cols]).astype(F32)
                     z = term if z is None else z + term
                 z1e[s + r:s + r + g, :, cols] = z.reshape(g, Q, H).astype(BF16)
@@ -537,8 +540,7 @@
 
     def activate2(i, h2):
         s = order2[i]
-        g = divisor(b2, 8)
-        for r in range(0, b2, g):
+        for r, g in groups(b2, 8):
             sl = gelu_terms(h2[r * Q:(r + g) * Q, :])[1]
             d = ce[s + r:s + r + g].reshape(g * Q, C).astype(F32) * sl
             dh2e[s + r:s + r + g] = d.astype(BF16).reshape(g, Q, C)
@@ -553,16 +555,15 @@
     def delta(i, dz, hs):
         s = order3[i]
         done = 0 if i == 0 else order3[i - 1] + b3
-        g = divisor(b3, 8)
-        for r in range(0, b3, g):
+        for r, g in groups(b3, 8):
             own = [b for b in range(s + r, s + r + g) if 1 <= b <= L and b >= done]
             for t in range(2):
                 cols = slice(t * H, (t + 1) * H)
                 d = dz[r * Q:(r + g) * Q, cols].astype(BF16)
                 for j in range(4):
                     where = slice(s + r + HZ - 1, s + r + g + HZ - 1)
-                    u = u_s[j, where, :, cols].reshape(g * Q, H)
-                    sl = s_s[j, where, :, cols].reshape(g * Q, H)
+                    u = u_s[j, where, t].reshape(g * Q, H)
+                    sl = s_s[j, where, t].reshape(g * Q, H)
                     hs[t, pl.ds(r * px + j, g * Q, stride=4), :] = (
                         d * pwb[j:j + 1, cols] * sl).astype(F32)
                     if own:
@@ -573,8 +574,7 @@
                             part = part + m[k]
                         gpa[j, :, cols] += part.astype(F32)
             for t in range(2):
-                cols = slice(t * H, (t + 1) * H)
-                dh1e[s + r:s + r + g, :, cols] = (
+                dh1e[s + r:s + r + g, t] = (
                     hs[t, r * px:(r + g) * px].astype(BF16).reshape(g, px, H))
 
     share = L // 4
@@ -583,7 +583,9 @@
     def turn(upto):
         while turned[0] < L // bt and (turned[0] + 1) * bt + 1 <= upto:
             i = turned[0]
-            dt[:, i * bt * px:(i + 1) * bt * px] = dh1e[1 + i * bt:1 + (i + 1) * bt].reshape(bt * px, C).T
+            for t in range(2):
+                part = dh1e[1 + i * bt:1 + (i + 1) * bt, t].reshape(bt * px, H)
+                dt[t * H:(t + 1) * H, i * bt * px:(i + 1) * bt * px] = part.T
             turned[0] += 1
 
     turned = [0]
@@ -599,52 +601,56 @@
             first_sum[0]([acc1[:, k * C:(k + 1) * C] + g[:, k * C:(k + 1) * C] for k in range(3)])
 
     def input_gradient_of(b, n):
-        g = dot(stacked(dh1e, [b + 1 + D1, b + 1, b + 1 - D1], n), w1t[...])
+        parts = [dh1e[pl.ds(at, n), t].reshape(n * px, H)
+                 for at in (b + 1 + D1, b + 1, b + 1 - D1) for t in range(2)]
+        g = dot(jnp.concatenate(parts, axis=-1), w1t[...])
         dx_ref[pl.ds(b, n)] = g.astype(BF16).reshape(n, px, C)
 
     first.wait()
     steps = len(order1)
     hs = [hs_a, hs_b]
-    for i in range(steps + 1):
-        if i < steps:
-            if i == inner1:
-                for c in halos():
-                    c.wait()
-            mix(i, hs[i % 2])
+    h2 = [h2_a, h2_b]
+    for i in range(steps):
+        if i == inner1:
+            for c in halos():
+                c.wait()
+        if i == min(2, steps - 1):
+            for c in second:
+                c.wait()
+        mix(i, hs[i % 2])
         if i == 0:
             pl.semaphore_wait(barrier, len(targets))
             for c in halos():
                 c.start()
-        if i == 2:
-            for c in second:
-                c.wait()
+        if i == min(2, steps - 1):
             turn_weights(w1, w2, w1t, w2t)
         if i:
             activate(i - 1, hs[(i - 1) % 2])
 
-    @pl.when(core == 0)
-    def _():
-        z1e[pl.ds(0, HZ)] = jnp.zeros((HZ, Q, C), BF16)
-
-    @pl.when(core == 1)
-    def _():
-        z1e[pl.ds(HZ + L, HZ)] = jnp.zeros((HZ, Q, C), BF16)
-
-    h2 = [h2_a, h2_b]
-    for i in range(len(order2) + 1):
-        if i < len(order2):
-            mix2(i, h2[i % 2])
-        if i:
-            activate2(i - 1, h2[(i - 1) % 2])
+    reach = order2[0] + b2 + 2 * D2
+    apart = order1[-1] + b1 <= order2[0] or reach <= order1[-1]
+    early = apart and order2[0] >= HZ and reach <= HZ + L
+    if early:
+        mix2(0, h2[0])
+    activate(steps - 1, hs[(steps - 1) % 2])
+    z1e[pl.ds(jnp.where(core == 0, 0, HZ + L), HZ)] = jnp.zeros((HZ, Q, C), BF16)
+    if not early:
+        mix2(0, h2[0])
+    for i in range(len(order2)):
+        if i + 1 < len(order2):
+            mix2(i + 1, h2[(i + 1) % 2])
+        activate2(i, h2[i % 2])
 
     dz = [dz_a, dz_b]
     mix3(0, dz[0])
     d2 = dh2e[pl.ds(HC, L)].reshape(L * Q, C)
     acc2 = dot_rows(d2, stacked(z1e, [HZ - D2, HZ, HZ + D2], L))
+    delta(0, dz[0], hs[0])
     second_sum[0]([acc2[:, k * C:(k + 1) * C] for k in range(3)])
     count = len(order3)
     for i in range(count):
-        delta(i, dz[i % 2], hs[i % 2])
+        if i:
+            delta(i, dz[i % 2], hs[i % 2])
         if i + 1 < count:
             mix3(i + 1, dz[(i + 1) % 2])
             turn(order3[i] + b3)
@@ -652,20 +658,11 @@
         if i == 1:
             second_sum[1]()
 
-    patch_a()
-
-    @pl.when(core == 0)
-    def _():
-        dh1e[0] = jnp.zeros((px, C), BF16)
-
-    @pl.when(core == 1)
-    def _():
-        dh1e[L + 1] = jnp.zeros((px, C), BF16)
-
     turn(n3)
     first_gradient(3)
-    patch_b()
-    after = [[], [first_sum[1]], [second_sum[2], patch_c], []]
+    patch_a()
+    dh1e[jnp.where(core == 0, 0, L + 1)] = jnp.zeros((2, px, H), BF16)
+    after = [[patch_b], [first_sum[1]], [second_sum[2], patch_c], []]
 
     def put(q):
         def row(k, value):
@@ -715,10 +712,10 @@
         pltpu.VMEM((L + 2 * HC, Q, C), BF16),
         pltpu.VMEM((L + 2 * HZ, Q, C), BF16),
         pltpu.VMEM((L + 2 * HC, Q, C), BF16),
-        pltpu.VMEM((L + 2, px, C), BF16),
+        pltpu.VMEM((L + 2, 2, px, H), BF16),
         pltpu.VMEM((C, L * px), BF16),
-        pltpu.VMEM((4, L + 2 * HZ, Q, C), BF16),
-        pltpu.VMEM((4, L + 2 * HZ, Q, C), BF16),
+        pltpu.VMEM((4, L + 2 * HZ, 2, Q, H), BF16),
+        pltpu.VMEM((4, L + 2 * HZ, 2, Q, H), BF16),
         pltpu.VMEM((2, wide * px, H), F32),
         pltpu.VMEM((2, wide * px, H), F32),
         pltpu.VMEM((b2 * Q, C), F32),

time: 37.6 us -> 37 us (0.984)
  Pallas kernels: 36.6 us -> 36 us
    pallas_call x1, Pallas kernels: 34.1 us -> 33.5 us  [step_pass(): pl.pallas_call(functools.partial(step_kernel, scale, lo_n, hi_n), out_sha...]
where the time goes in v3:
time: 37 us; the launch traced here: 36.8 us
  Pallas kernels  36 us (97%)
  between operations  0.8 us (2%)
    pallas_call x1, Pallas kernels, step_pass(): pl.pallas_call(functools.partial(step_kernel, scale, lo_n, hi_n), out_sha...  33.5 us
    pallas_call x1, Pallas kernels, hand_over(): pl.pallas_call(functools.partial(hand_over_kernel, n), out_shape=(jax.Sha...  2.5 us

profile of v3, /device:TPU:0, one launch (start us, length us, event | category | flops | bytes accessed | tf_op | source)
XLA Modules:
  0.0 36.8 jit_solution(9040275035315882829)
XLA Ops:
  0.6 33.5 %step_pass.1 = (bf16[112,64,256]{2,1,0:T(8,128)(2,1)S(1)}, f32[2,3,16,256]{3,2,1,0:T(8,128)S(1)}, f32[4,256]{1,0:T(4,128)S(1)}) custom-call(bf16[112,64,256]{2,1,0:T(8,128)(2,1)} %x_hbm.1, bf16[112,16,256]{2,1,0:T(8,128)(2,1)} %cot_hbm.1, bf16[3,256,256]{2,1,0:T(8,128)(2,1)} %w1_hbm.1, bf16[3,256,256]{2,1,0:T(8,128)(2,1)} %w2_hbm.1, f32[4,256]{1,0:T(4,128)} %pw_ref.1), custom_call_target="tpu_custom_call" | custom-call | tf_op jit(solution)/shard_map/step_pass/pallas_call | solution.py:747
  34.1 2.5 %hand_over.1 = (bf16[112,64,256]{2,1,0:T(8,128)(2,1)}, f32[3,16,256]{2,1,0:T(8,128)}, f32[3,16,256]{2,1,0:T(8,128)}, f32[4,256]{1,0:T(4,128)}) custom-call(bf16[112,64,256]{2,1,0:T(8,128)(2,1)S(1)} %get-tuple-element.11.dx_ref, f32[2,3,16,256]{3,2,1,0:T(8,128)S(1)} %get-tuple-element.12.o_ref, f32[4,256]{1,0:T(4,128)S(1)} %get-tuple-element.13.p_ref), custom_call_target="tpu_custom_call" | custom-call | tf_op jit(solution)/shard_map/hand_over/pallas_call | solution.py:781

commit v4 on v3

--- a/solution.py
+++ b/solution.py
@@ -333,7 +333,7 @@
 
 def first_plan(L):
     n1 = L + 2 * HZ
-    size, starts = blocks(n1, min(6, n1))
+    size, starts = blocks(n1, min(5, n1))
     inner, outer = inner_first(starts, size, n1, HZ)
     order = inner + outer
     return n1, size, order, len(inner), fresh(order, size, 2 * D1, HX, HX + L)

time: 37 us -> 36.4 us (0.984)
  Pallas kernels: 36 us -> 35.4 us
    pallas_call x1, Pallas kernels: 33.5 us -> 32.9 us  [step_pass(): pl.pallas_call(functools.partial(step_kernel, scale, lo_n, hi_n), out_sha...]
where the time goes in v4:
time: 36.4 us; the launch traced here: 36.2 us
  Pallas kernels  35.4 us (97%)
  between operations  0.8 us (2%)
    pallas_call x1, Pallas kernels, step_pass(): pl.pallas_call(functools.partial(step_kernel, scale, lo_n, hi_n), out_sha...  32.9 us
    pallas_call x1, Pallas kernels, hand_over(): pl.pallas_call(functools.partial(hand_over_kernel, n), out_shape=(jax.Sha...  2.5 us

profile of v4, /device:TPU:0, one launch (start us, length us, event | category | flops | bytes accessed | tf_op | source)
XLA Modules:
  0.0 36.2 jit_solution(4415638256756908442)
XLA Ops:
  0.6 32.9 %step_pass.1 = (bf16[112,64,256]{2,1,0:T(8,128)(2,1)S(1)}, f32[2,3,16,256]{3,2,1,0:T(8,128)S(1)}, f32[4,256]{1,0:T(4,128)S(1)}) custom-call(bf16[112,64,256]{2,1,0:T(8,128)(2,1)} %x_hbm.1, bf16[112,16,256]{2,1,0:T(8,128)(2,1)} %cot_hbm.1, bf16[3,256,256]{2,1,0:T(8,128)(2,1)} %w1_hbm.1, bf16[3,256,256]{2,1,0:T(8,128)(2,1)} %w2_hbm.1, f32[4,256]{1,0:T(4,128)} %pw_ref.1), custom_call_target="tpu_custom_call" | custom-call | tf_op jit(solution)/shard_map/step_pass/pallas_call | solution.py:747
  33.6 2.5 %hand_over.1 = (bf16[112,64,256]{2,1,0:T(8,128)(2,1)}, f32[3,16,256]{2,1,0:T(8,128)}, f32[3,16,256]{2,1,0:T(8,128)}, f32[4,256]{1,0:T(4,128)}) custom-call(bf16[112,64,256]{2,1,0:T(8,128)(2,1)S(1)} %get-tuple-element.11.dx_ref, f32[2,3,16,256]{3,2,1,0:T(8,128)S(1)} %get-tuple-element.12.o_ref, f32[4,256]{1,0:T(4,128)S(1)} %get-tuple-element.13.p_ref), custom_call_target="tpu_custom_call" | custom-call | tf_op jit(solution)/shard_map/hand_over/pallas_call | solution.py:781
